TPU v7x, 128 devices: a whole 4x4x4 slice. The times are simulated.
128 devices in a mesh: leaf: 128 (over y, z, x, core).
Axes of the slice: x: 4, y: 4, z: 4, core: 2. Of those that a mesh axis runs over, the one named last changes fastest.
Arguments:
- density: bfloat16 [131072, 220], P('leaf'), may hold values from -6 to 6
- vel_mask: int32 [131072], P('leaf'), may hold values from 0 to 1, as said below
- near_list: int32 [131072, 27], P('leaf'), may hold values from 0 to 131071, as said below
- near_ops: bfloat16 [27, 220, 660], replicated, may hold values from -0.078125 to 0.078125
- upward_ops: bfloat16 [8, 220, 56], replicated, may hold values from -0.0068359375 to 0.0068359375
- coupling_operators: float32 [56, 168], replicated, may hold values from -0.75 to 0.75
- coarse_weights: float32 [32, 32], replicated, may hold values from -1 to 1
- downward_ops: bfloat16 [8, 56, 220], replicated, may hold values from -0.75 to 0.75
- conc_owner: int32 [131072, 1], P('leaf'), may hold values from 0 to 127; in each aligned block of 1024 rows (0 to 1023, 1024 to 2047, ...) at most 16 rows name the same one
- concentration: bfloat16 [262144, 220], P('leaf'), may hold values from -6 to 6
- departure: int32 [262144], P('leaf'), may hold values from 0 to 2047
- departure_class: int32 [262144], P('leaf'), may hold values from 0 to 7
- shift_ops: bfloat16 [8, 220, 220], replicated, may hold values from -0.4375 to 0.4375
- eval_ops: bfloat16 [220, 1024], replicated, may hold values from -0.4375 to 0.4375
Outputs:
- velocity: bfloat16 [131072, 660], P('leaf')
- advected: bfloat16 [262144, 256], P('leaf')
Inputs may be any that keep to these rules, and one draw needn't show every extreme that they name: `vel_mask`: in each aligned block of 1024 rows the real leaves come first; every block has from 341 to 1024 real leaves, and both counts occur in every draw. `near_list`: entry [i, t] lies within 1024 of i; column 13 is i itself. `conc_owner`: in each aligned block of 1024 rows, the rows of one device, no owner is named more than 16 times, a bound that some block reaches. `departure`: A slot index within the same device's 2048 slots.
All inputs are finite; a program needn't handle non-finite values.
Results may differ from a plain program's by a relative error of at most 0.008.
Values may be sent and summed in bfloat16 or wider, within the bound.
No kernel may reach another device: no remote copies, remote signals or barrier semaphores. Data moves between devices by JAX's collectives and lax.ppermute only.
A program may use at most 128 MiB of HBM per device.

v0:
```python
import jax
import jax.numpy as jnp
from jax import lax
from jax.sharding import PartitionSpec as P

SPAN = 4
time_step = 0.5


def with_halo(block, sides, width):
    for axis, dim in sides:
        count = lax.axis_size(axis)
        forward = [(i, i + 1) for i in range(count - 1)]
        backward = [(target, source) for source, target in forward]
        low = lax.ppermute(
            lax.slice_in_dim(block, block.shape[dim] - width, None, axis=dim), axis, forward
        )
        high = lax.ppermute(lax.slice_in_dim(block, 0, width, axis=dim), axis, backward)
        block = jnp.concatenate([low, block, high], axis=dim)
    return block


def shifted_rows(gathered, classes, shift_ops):
    kinds = shift_ops.shape[0]
    total = jnp.zeros((gathered.shape[0], shift_ops.shape[2]), jnp.float32)
    for kind in range(kinds):
        product = jnp.dot(gathered, shift_ops[kind], preferred_element_type=jnp.float32)
        total = jnp.where((classes == kind)[:, None], product, total)
    return total.astype(jnp.bfloat16)


def advect_rows(base, velocity_rows, alive_rows, eval_ops):
    value_rows = jnp.dot(base, eval_ops, preferred_element_type=jnp.float32)
    nodes_count = value_rows.shape[1] // 4
    speeds = jnp.dot(
        velocity_rows.reshape(-1, eval_ops.shape[0]),
        eval_ops[:, :nodes_count],
        preferred_element_type=jnp.float32,
    )
    speeds = speeds.reshape(base.shape[0], 3, nodes_count)
    correction = speeds[:, 0] * value_rows[:, nodes_count : 2 * nodes_count]
    correction = correction + speeds[:, 1] * value_rows[:, 2 * nodes_count : 3 * nodes_count]
    correction = correction + speeds[:, 2] * value_rows[:, 3 * nodes_count :]
    return (alive_rows[:, None] * (value_rows[:, :nodes_count] - time_step * correction)).astype(
        jnp.bfloat16
    )


def local(
    density,
    vel_mask,
    near_list,
    near_ops,
    upward_ops,
    coupling_operators,
    coarse_weights,
    downward_ops,
    conc_owner,
    concentration,
    departure,
    departure_class,
    shift_ops,
    eval_ops,
):
    leaves = density.shape[0]
    coef_width = density.shape[1]
    devices = lax.axis_size("leaf")
    my_index = lax.axis_index("leaf")
    alive = vel_mask.astype(jnp.float32)
    live_density = (density.astype(jnp.float32) * alive[:, None]).astype(jnp.bfloat16)
    padded = with_halo(live_density, (("leaf", 0),), leaves)
    local_rows = near_list - my_index * leaves + leaves

    def near_step(position, total):
        rows = lax.dynamic_index_in_dim(local_rows, position, 1, keepdims=False)
        picked = jnp.take(padded, rows, axis=0)
        operator = lax.dynamic_index_in_dim(near_ops, position, 0, keepdims=False)
        return total + jnp.dot(picked, operator, preferred_element_type=jnp.float32)

    nearby_field = lax.fori_loop(
        0, near_ops.shape[0], near_step, jnp.zeros((leaves, 3 * coef_width), jnp.float32)
    )
    parts = jnp.einsum(
        "gop,opq->goq",
        live_density.reshape(-1, 8, coef_width),
        upward_ops,
        preferred_element_type=jnp.float32,
    )
    own_part = jnp.sum(parts, axis=(0, 1))
    boxes = devices // SPAN
    my_box = my_index // SPAN
    box_rows = (jnp.arange(boxes, dtype=jnp.int32) == my_box).astype(jnp.float32)
    moments = lax.psum(box_rows[:, None] * own_part[None, :], "leaf")
    expanded = jnp.dot(moments, coupling_operators, precision=lax.Precision.HIGHEST)
    weight_row = lax.dynamic_slice_in_dim(coarse_weights, my_box, 1, 0)
    own_expansion = jnp.dot(weight_row, expanded, precision=lax.Precision.HIGHEST)
    box_far = jnp.einsum(
        "jq,oqp->ojp",
        own_expansion.reshape(3, -1),
        downward_ops.astype(jnp.float32),
        precision=lax.Precision.HIGHEST,
    )
    far_field = jnp.broadcast_to(
        box_far.reshape(1, 8, 3 * coef_width), (leaves // 8, 8, 3 * coef_width)
    ).reshape(leaves, 3 * coef_width)
    velocity = ((nearby_field + far_field) * alive[:, None]).astype(jnp.bfloat16)
    slots_here = concentration.shape[0]
    capacity = slots_here // devices
    owner = conc_owner[:, 0]
    onehot = (owner[:, None] == jnp.arange(devices, dtype=jnp.int32)[None, :]).astype(jnp.int32)
    rank = jnp.sum(jnp.cumsum(onehot, axis=0) * onehot, axis=1) - 1
    send_slot = owner * capacity + rank
    placement = (jnp.arange(slots_here, dtype=jnp.int32)[:, None] == send_slot[None, :]).astype(
        jnp.bfloat16
    )
    send_velocity = jnp.dot(placement, velocity, preferred_element_type=jnp.float32).astype(
        jnp.bfloat16
    )
    send_alive = jnp.dot(
        placement, vel_mask.astype(jnp.bfloat16), preferred_element_type=jnp.float32
    ).astype(jnp.bfloat16)
    got_velocity, got_alive = (
        lax.all_to_all(
            send_velocity.reshape(devices, capacity, -1),
            "leaf",
            split_axis=0,
            concat_axis=0,
            tiled=True,
        ),
        lax.all_to_all(
            send_alive.reshape(devices, capacity), "leaf", split_axis=0, concat_axis=0, tiled=True
        ),
    )
    base = shifted_rows(concentration[departure], departure_class, shift_ops)
    advected = advect_rows(
        base,
        got_velocity.reshape(slots_here, -1),
        got_alive.reshape(slots_here).astype(jnp.float32),
        eval_ops,
    )
    return (velocity, advected)


def solution(mesh):
    placed = (
        P("leaf", None),
        P("leaf"),
        P("leaf", None),
        P(),
        P(),
        P(),
        P(),
        P(),
        P("leaf", None),
        P("leaf", None),
        P("leaf"),
        P("leaf"),
        P(),
        P(),
    )
    return jax.shard_map(
        local,
        mesh=mesh,
        in_specs=placed,
        out_specs=(P("leaf", None), P("leaf", None)),
        check_vma=False,
    )
```

profile of v0, /device:TPU:1, one launch (start us, length us, event | category | flops | bytes accessed | tf_op | source)
XLA Modules:
  0.0 428.8 jit_solution(9726396116737616334)
XLA Ops:
  13.9 14.0 %all-to-all-start = ((bf16[128,1,16]{2,1,0:T(2,128)(2,1)}), bf16[128,1,16]{2,1,0:T(2,128)(2,1)S(1)}, u32[]{:S(2)}, u32[]{:S(2)}) async-start(bf16[128,1,16]{2,1,0:T(2,128)(2,1)} %all_to_all.12), calls=%async_computation | async-start | bytes 131072 | tf_op jit(solution)/shard_map/all_to_all | solution.py:130
  28.7 67.2 %psum.7 = f32[32,56]{1,0:T(8,128)S(1)} all-reduce(f32[32,56]{1,0:T(8,128)S(1)} %broadcast_multiply_fusion), channel_id=1, replica_groups=mesh['leaf'=128] {'leaf'}, use_global_device_ids=true, to_apply=%region_3.4 | all-reduce | flops 1792 | bytes 14336 | tf_op jit(solution)/shard_map/psum | solution.py:93
  99.5 7.5 %gather_fusion.1 = bf16[2048,220]{1,0:T(8,128)(2,1)S(1)} fusion(bf16[2048,220]{1,0:T(8,128)(2,1)S(1)} %copy.42, s32[2048]{0:T(1024)S(1)} %fusion.46), kind=kCustom, calls=%fused_computation.1 | custom fusion | bytes 1810432 | tf_op jit(solution)/shard_map/gather | solution.py:134
  111.1 237.2 %while.14 = (s32[]{:T(128)}, f32[1024,660]{0,1:T(8,128)}, s32[1024,27]{0,1:T(8,128)}, bf16[3072,220]{1,0:T(8,128)(2,1)S(1)}, bf16[27,220,660]{1,2,0:T(8,128)(2,1)}, /*index=5*/s32[]{:T(128)}, s32[]{:T(128)}) while((s32[]{:T(128)}, f32[1024,660]{0,1:T(8,128)}, s32[1024,27]{0,1:T(8,128)}, bf16[3072,220]{1,0:T(8,128)(2,1)S(1)}, ...), condition=%wide.region_1.2_spmd.clone, body=%wide.region_0.1_spmd.clone.sunk | while | flops 298953728 | bytes 7137383 | solution.py:80
  111.9 3.9 gather_fusion
  119.8 3.9 gather_fusion
  123.7 4.1 select_add_fusion.2
  128.6 3.9 gather_fusion
  132.5 4.1 select_add_fusion.2
  137.4 3.9 gather_fusion
  141.4 4.1 select_add_fusion.2
  146.2 3.9 gather_fusion
  150.2 4.1 select_add_fusion.2
  155.0 3.9 gather_fusion
  159.0 4.1 select_add_fusion.2
  163.9 3.9 gather_fusion
  167.8 4.1 select_add_fusion.2
  172.7 3.9 gather_fusion
  176.6 4.1 select_add_fusion.2
  181.5 3.9 gather_fusion
  185.4 4.1 select_add_fusion.2
  190.3 3.9 gather_fusion
  194.3 4.1 select_add_fusion.2
  203.1 4.1 select_add_fusion.2
  207.9 3.9 gather_fusion
  211.9 4.1 select_add_fusion.2
  220.7 4.1 select_add_fusion.2
  229.5 4.1 select_add_fusion.2
  238.3 4.1 select_add_fusion.2
  247.2 4.1 select_add_fusion.2
  256.0 4.1 select_add_fusion.2
  264.8 4.1 select_add_fusion.2
  273.6 4.1 select_add_fusion.2
  282.4 4.1 select_add_fusion.2
  291.3 4.1 select_add_fusion.2
  300.1 4.1 select_add_fusion.2
  308.9 4.1 select_add_fusion.2
  317.7 4.1 select_add_fusion.2
  326.5 4.1 select_add_fusion.2
  335.3 4.1 select_add_fusion.2
  344.2 4.1 select_add_fusion.2
  353.9 4.5 %fusion.11 = bf16[2048,660]{0,1:T(8,128)(2,1)} fusion(bf16[1024,660]{1,0:T(8,128)(2,1)S(1)} %fusion.13, s32[1024]{0:T(1024)S(1)} %add_add_fusion), kind=kOutput, calls=%fused_computation.18 | convolution fusion | flops 2771689472 | bytes 4059136 | tf_op jit(solution)/shard_map/dot_general | solution.py:116
  358.3 4.6 %copy.51 = bf16[2048,660]{1,0:T(8,128)(2,1)} copy(bf16[2048,660]{0,1:T(8,128)(2,1)} %fusion.11) | data formatting | bytes 5406720 | tf_op jit(solution)/shard_map/convert_element_type | solution.py:116
  363.0 5.7 %all-to-all-start.1 = ((bf16[128,16,660]{2,1,0:T(8,128)(2,1)}), bf16[128,16,660]{2,1,0:T(8,128)(2,1)}, u32[]{:S(2)}, u32[]{:S(2)}) async-start(bf16[128,16,660]{2,1,0:T(8,128)(2,1)} %bitcast.102), calls=%async_computation.1 | async-start | bytes 6291456 | tf_op jit(solution)/shard_map/all_to_all | solution.py:123
  374.9 6.4 %fusion.28 = f32[2048,1024]{1,0:T(8,128)} fusion(bf16[220,1024]{1,0:T(8,128)(2,1)S(1)} %copy-done.4, bf16[2048,220]{0,1:T(8,128)(2,1)} %fusion.41, bf16[2048,220]{0,1:T(8,128)(2,1)} %fusion.19, bf16[2048,220]{1,0:T(8,128)(2,1)S(1)} %gather_fusion.1, pred[2048]{0:T(1024)(128)(4,1)S(1)} %get-tuple-element.144, pred[2048]{0:T(1024)(128)(4,1)S(1)} %get-tuple-element.139, ...), kind=kOutput, calls=%fused_computation.46 | convolution fusion | flops 1121894400 | bytes 11643424 | tf_op jit(solution)/shard_map/dot_general | solution.py:33
  383.1 27.0 %all-to-all-done.1 = bf16[128,16,660]{2,1,0:T(8,128)(2,1)} async-done(((bf16[128,16,660]{2,1,0:T(8,128)(2,1)}), bf16[128,16,660]{2,1,0:T(8,128)(2,1)}, u32[]{:S(2)}, u32[]{:S(2)}) %all-to-all-start.1) | async-done | bytes 2703392 | tf_op jit(solution)/shard_map/all_to_all | solution.py:123
  410.1 10.8 %dot_general.78 = bf16[2048,3,220]{2,1,0:T(4,128)(2,1)} reshape(bf16[128,16,660]{2,1,0:T(8,128)(2,1)} %all-to-all-done.1) | data formatting | bytes 5406720 | tf_op jit(solution)/shard_map/dot_general | solution.py:35
  424.1 4.6 %fusion.26 = bf16[2048,256]{1,0:T(8,128)(2,1)} fusion(f32[2048,1024]{1,0:T(8,128)} %fusion.28, f32[2048,3,256]{2,0,1:T(8,128)S(1)} %fusion.14, f32[2048]{0:T(1024)S(1)} %reshape.89), kind=kLoop, calls=%fused_computation.38 | loop fusion | flops 4718592 | bytes 15736832 | tf_op jit(solution)/shard_map/convert_element_type | solution.py:44
  (155 shorter events, 125.8 us)
Async XLA Ops:
  0.6 96.4 %copy-start = (bf16[8,56,220]{2,1,0:T(8,128)(2,1)S(1)}, bf16[8,56,220]{2,1,0:T(8,128)(2,1)}, u32[]{:S(2)}) copy-start(bf16[8,56,220]{2,1,0:T(8,128)(2,1)} %param.23) | copy-start | bytes 591364
  0.6 10.6 %copy-start.13 = (s32[1024,1]{0,1:T(1,128)S(1)}, s32[1024,1]{0,1:T(1,128)}, u32[]{:S(2)}) copy-start(s32[1024,1]{0,1:T(1,128)} %param.24) | copy-start | bytes 12292
  3.6 105.8 %collective-permute-start.1 = (bf16[1024,220]{1,0:T(8,128)(2,1)}, bf16[1024,220]{1,0:T(8,128)(2,1)}, u32[]{:S(2)}, u32[]{:S(2)}) collective-permute-start(bf16[1024,220]{1,0:T(8,128)(2,1)} %multiply_convert_fusion), channel_id=1, source_target_pairs={{1,0},{2,1},{3,2},{4,3},{5,4},{6,5},{7,6},{8,7},{9,8},{10,9},{11,1... | collective-permute-start | bytes 1351688 | tf_op jit(solution)/shard_map/ppermute | solution.py:18
  6.9 102.5 %collective-permute-start = (bf16[1024,220]{1,0:T(8,128)(2,1)}, bf16[1024,220]{1,0:T(8,128)(2,1)}, u32[]{:S(2)}, u32[]{:S(2)}) collective-permute-start(bf16[1024,220]{1,0:T(8,128)(2,1)} %multiply_convert_fusion), channel_id=1, source_target_pairs={{0,1},{1,2},{2,3},{3,4},{4,5},{5,6},{6,7},{7,8},{8,9},{9,10},{10,1... | collective-permute-start | bytes 1351688 | tf_op jit(solution)/shard_map/ppermute | solution.py:15
  11.3 16.9 %copy-start.15 = (s32[2048]{0:T(1024)S(1)}, s32[2048]{0:T(1024)}, u32[]{:S(2)}) copy-start(s32[2048]{0:T(1024)} %param.26) | copy-start | bytes 24580
  11.3 16.9 %copy-start.14 = (s32[2048]{0:T(1024)S(1)}, s32[2048]{0:T(1024)}, u32[]{:S(2)}) copy-start(s32[2048]{0:T(1024)} %param.27) | copy-start | bytes 24580
  11.3 16.9 %copy-start.16 = (bf16[8,220,56]{1,2,0:T(8,128)(2,1)S(1)}, bf16[8,220,56]{1,2,0:T(8,128)(2,1)}, u32[]{:S(2)}) copy-start(bf16[8,220,56]{1,2,0:T(8,128)(2,1)} %param.20) | copy-start | bytes 591364
  11.7 84.2 %copy-start.12 = (f32[56,168]{1,0:T(8,128)S(1)}, f32[56,168]{1,0:T(8,128)}, u32[]{:S(2)}) copy-start(f32[56,168]{1,0:T(8,128)} %param.21) | copy-start | bytes 112900
  11.7 85.7 %copy-start.3 = (bf16[2048,220]{0,1:T(8,128)(2,1)S(1)}, bf16[2048,220]{0,1:T(8,128)(2,1)}, u32[]{:S(2)}) copy-start(bf16[2048,220]{0,1:T(8,128)(2,1)} %param.25) | copy-start | bytes 2703364
  13.9 349.1 %all-to-all-start = ((bf16[128,1,16]{2,1,0:T(2,128)(2,1)}), bf16[128,1,16]{2,1,0:T(2,128)(2,1)S(1)}, u32[]{:S(2)}, u32[]{:S(2)}) async-start(bf16[128,1,16]{2,1,0:T(2,128)(2,1)} %all_to_all.12), calls=%async_computation | async-start | bytes 131072 | tf_op jit(solution)/shard_map/all_to_all | solution.py:130
  99.5 7.5 %copy-start.2 = (bf16[8,220,220]{2,0,1:T(8,128)(2,1)S(1)}, bf16[8,220,220]{2,0,1:T(8,128)(2,1)}, u32[]{:S(2)}) copy-start(bf16[8,220,220]{2,0,1:T(8,128)(2,1)} %param.28) | copy-start | bytes 2323204
  363.0 5.7 %copy-start.9 = (bf16[1,220,220]{2,0,1:T(2,128)(2,1)S(1)}, bf16[1,220,220]{2,0,1:T(2,128)(2,1)}, u32[]{:S(2)}) copy-start(bf16[1,220,220]{2,0,1:T(2,128)(2,1)} %get-tuple-element.132) | copy-start | bytes 290404
  363.0 6.2 %copy-start.8 = (bf16[1,220,220]{2,0,1:T(2,128)(2,1)S(1)}, bf16[1,220,220]{2,0,1:T(2,128)(2,1)}, u32[]{:S(2)}) copy-start(bf16[1,220,220]{2,0,1:T(2,128)(2,1)} %get-tuple-element.133) | copy-start | bytes 290404
  363.0 47.1 %all-to-all-start.1 = ((bf16[128,16,660]{2,1,0:T(8,128)(2,1)}), bf16[128,16,660]{2,1,0:T(8,128)(2,1)}, u32[]{:S(2)}, u32[]{:S(2)}) async-start(bf16[128,16,660]{2,1,0:T(8,128)(2,1)} %bitcast.102), calls=%async_computation.1 | async-start | bytes 6291456 | tf_op jit(solution)/shard_map/all_to_all | solution.py:123
  368.6 1.1 copy-start.7
  368.7 1.6 copy-start.6
  369.2 1.6 copy-start.5
  369.8 2.5 copy-start.11
  372.3 0.9 copy-start.10
  372.9 2.0 copy-start.4
  424.1 4.6 %copy-start.1 = (bf16[8,56,220]{2,1,0:T(8,128)(2,1)S(1)}, bf16[8,56,220]{2,1,0:T(8,128)(2,1)}, u32[]{:S(2)}) copy-start(bf16[8,56,220]{2,1,0:T(8,128)(2,1)} %param.23) | copy-start | bytes 591364
where the time goes:
time: 432 us; the launch traced here: 429 us
  local copies, waits for them, and re-layouts  141 us (33%)
  matrix products  132 us (31%)
  blocking collectives  67.2 us (16%)
  other arithmetic  34.3 us (8%)
  waiting for transfers between devices  27 us (6%)
  starting transfers between devices  26.1 us (6%)
    dot_general x27, matrix products, near_step(): return total + jnp.dot(picked, operator, preferred_element_type=jnp.float32)  109 us
    gather x27, local copies, waits for them, and re-layouts, near_step(): picked = jnp.take(padded, rows, axis=0)  106 us
    psum x1, blocking collectives, local(): moments = lax.psum(box_rows[:, None] * own_part[None, :], 'leaf')  67.2 us
    all_to_all x1, waiting for transfers between devices, local(): lax.all_to_all(send_velocity.reshape(devices, capacity, -1), 'leaf', spli...  27 us
    and x27, other arithmetic, near_step(): picked = jnp.take(padded, rows, axis=0)  21.3 us
    all_to_all x1, starting transfers between devices, local(): lax.all_to_all(send_alive.reshape(devices, capacity), 'leaf', split_axis=...  14 us
    dot_general x1, local copies, waits for them, and re-layouts, advect_rows(): jnp.dot(velocity_rows.reshape(-1, eval_ops.shape[0]), eval_ops[:, :nodes_...  10.8 us
  transfers between devices with their start and end apart: 4, of which 1 were waited for; matrix products, arithmetic and copies ran while one was open for 66% of the time, Pallas kernels for 0%

commit v1 on v0

--- a/solution.py
+++ b/solution.py
@@ -90,7 +90,7 @@
     boxes = devices // SPAN
     my_box = my_index // SPAN
     box_rows = (jnp.arange(boxes, dtype=jnp.int32) == my_box).astype(jnp.float32)
-    moments = lax.psum(box_rows[:, None] * own_part[None, :], "leaf")
+    moments = jnp.sum(lax.all_gather(box_rows[:, None] * own_part[None, :], "leaf"), axis=0)
     expanded = jnp.dot(moments, coupling_operators, precision=lax.Precision.HIGHEST)
     weight_row = lax.dynamic_slice_in_dim(coarse_weights, my_box, 1, 0)
     own_expansion = jnp.dot(weight_row, expanded, precision=lax.Precision.HIGHEST)

time: 432 us -> 409 us (0.947)
  blocking collectives: 67.2 us -> 41.8 us
    psum x1 -> x0, blocking collectives: 67.2 us -> none  [local(): moments = lax.psum(box_rows[:, None] * own_part[None, :], 'leaf')]
    all_gather x0 -> x1, blocking collectives: none -> 41.8 us  [local(): lax.all_gather(box_rows[:, None] * own_part[None, :], 'leaf')]
  transfers between devices with their start and end apart: 4 -> 4, of which waited for: 1 -> 1; matrix products, arithmetic and copies ran while one was open for 66% -> 71% of each run, Pallas kernels for 0% -> 0%
where the time goes in v1:
time: 409 us; the launch traced here: 406 us
  local copies, waits for them, and re-layouts  141 us (34%)
  matrix products  133 us (33%)
  blocking collectives  41.8 us (10%)
  other arithmetic  35.2 us (9%)
  waiting for transfers between devices  26.9 us (7%)
  starting transfers between devices  26.5 us (6%)
    dot_general x27, matrix products, near_step(): return total + jnp.dot(picked, operator, preferred_element_type=jnp.float32)  109 us
    gather x27, local copies, waits for them, and re-layouts, near_step(): picked = jnp.take(padded, rows, axis=0)  106 us
    all_gather x1, blocking collectives, local(): lax.all_gather(box_rows[:, None] * own_part[None, :], 'leaf')  41.8 us
    all_to_all x1, waiting for transfers between devices, local(): lax.all_to_all(send_velocity.reshape(devices, capacity, -1), 'leaf', spli...  26.9 us
    and x27, other arithmetic, near_step(): picked = jnp.take(padded, rows, axis=0)  21.3 us
    all_to_all x1, starting transfers between devices, local(): lax.all_to_all(send_alive.reshape(devices, capacity), 'leaf', split_axis=...  14 us
    dot_general x1, local copies, waits for them, and re-layouts, advect_rows(): jnp.dot(velocity_rows.reshape(-1, eval_ops.shape[0]), eval_ops[:, :nodes_...  10.8 us
  transfers between devices with their start and end apart: 4, of which 1 were waited for; matrix products, arithmetic and copies ran while one was open for 71% of the time, Pallas kernels for 0%

profile of v1, /device:TPU:1, one launch (start us, length us, event | category | flops | bytes accessed | tf_op | source)
XLA Modules:
  0.0 405.5 jit_solution(11100500127124011335)
XLA Ops:
  13.9 14.0 %all-to-all-start = ((bf16[128,1,16]{2,1,0:T(2,128)(2,1)}), bf16[128,1,16]{2,1,0:T(2,128)(2,1)S(1)}, u32[]{:S(2)}, u32[]{:S(2)}) async-start(bf16[128,1,16]{2,1,0:T(2,128)(2,1)} %all_to_all.12), calls=%async_computation | async-start | bytes 131072 | tf_op jit(solution)/shard_map/all_to_all | solution.py:130
  30.2 41.8 %all_gather.4 = f32[128,32,56]{2,1,0:T(8,128)} all-gather(f32[1,32,56]{2,1,0:T(8,128)S(1)} %broadcast_multiply_fusion), channel_id=1, replica_groups=mesh['leaf'=128] {'leaf'}, dimensions={0}, use_global_device_ids=true | all-gather | bytes 924672 | tf_op jit(solution)/shard_map/all_gather | solution.py:93
  76.0 7.5 %gather_fusion.1 = bf16[2048,220]{1,0:T(8,128)(2,1)S(1)} fusion(bf16[2048,220]{1,0:T(8,128)(2,1)S(1)} %copy.42, s32[2048]{0:T(1024)S(1)} %fusion.46), kind=kCustom, calls=%fused_computation.1 | custom fusion | bytes 1810432 | tf_op jit(solution)/shard_map/gather | solution.py:134
  87.6 237.2 %while.14 = (s32[]{:T(128)}, f32[1024,660]{0,1:T(8,128)}, s32[1024,27]{0,1:T(8,128)}, bf16[3072,220]{1,0:T(8,128)(2,1)S(1)}, bf16[27,220,660]{1,2,0:T(8,128)(2,1)}, /*index=5*/s32[]{:T(128)}, s32[]{:T(128)}) while((s32[]{:T(128)}, f32[1024,660]{0,1:T(8,128)}, s32[1024,27]{0,1:T(8,128)}, bf16[3072,220]{1,0:T(8,128)(2,1)S(1)}, ...), condition=%wide.region_1.2_spmd.clone, body=%wide.region_0.1_spmd.clone.sunk | while | flops 298953728 | bytes 7137383 | solution.py:80
  88.4 3.9 gather_fusion
  96.3 3.9 gather_fusion
  100.2 4.1 %select_add_fusion.2 = f32[1024,660]{0,1:T(8,128)} fusion(f32[1024,660]{0,1:T(8,128)} %get-tuple-element.192, pred[]{:T(512)S(6)} %compare.5, bf16[1024,220]{1,0:T(8,128)(2,1)S(1)} %gather_fusion, pred[1024]{0:T(1024)(128)(4,1)S(1)} %get-tuple-element.183, bf16[27,220,660]{1,2,0:T(8,128)(2,1)} %get-tuple-element.202, s32[]{:T(128)S(6)} %copy.93), kind=kOutput, calls=%fused_computation.2.clone.1 | convolution fusion | flops 298946560 | bytes 6214661 | tf_op jit(solution)/shard_map/while/body/eval_jaxpr/dot_general | solution.py:78
  105.1 3.9 gather_fusion
  109.1 4.1 %select_add_fusion.2 = f32[1024,660]{0,1:T(8,128)} fusion(f32[1024,660]{0,1:T(8,128)} %get-tuple-element.192, pred[]{:T(512)S(6)} %compare.5, bf16[1024,220]{1,0:T(8,128)(2,1)S(1)} %gather_fusion, pred[1024]{0:T(1024)(128)(4,1)S(1)} %get-tuple-element.183, bf16[27,220,660]{1,2,0:T(8,128)(2,1)} %get-tuple-element.202, s32[]{:T(128)S(6)} %copy.93), kind=kOutput, calls=%fused_computation.2.clone.1 | convolution fusion | flops 298946560 | bytes 6214661 | tf_op jit(solution)/shard_map/while/body/eval_jaxpr/dot_general | solution.py:78
  113.9 3.9 gather_fusion
  117.9 4.1 %select_add_fusion.2 = f32[1024,660]{0,1:T(8,128)} fusion(f32[1024,660]{0,1:T(8,128)} %get-tuple-element.192, pred[]{:T(512)S(6)} %compare.5, bf16[1024,220]{1,0:T(8,128)(2,1)S(1)} %gather_fusion, pred[1024]{0:T(1024)(128)(4,1)S(1)} %get-tuple-element.183, bf16[27,220,660]{1,2,0:T(8,128)(2,1)} %get-tuple-element.202, s32[]{:T(128)S(6)} %copy.93), kind=kOutput, calls=%fused_computation.2.clone.1 | convolution fusion | flops 298946560 | bytes 6214661 | tf_op jit(solution)/shard_map/while/body/eval_jaxpr/dot_general | solution.py:78
  122.8 3.9 gather_fusion
  126.7 4.1 %select_add_fusion.2 = f32[1024,660]{0,1:T(8,128)} fusion(f32[1024,660]{0,1:T(8,128)} %get-tuple-element.192, pred[]{:T(512)S(6)} %compare.5, bf16[1024,220]{1,0:T(8,128)(2,1)S(1)} %gather_fusion, pred[1024]{0:T(1024)(128)(4,1)S(1)} %get-tuple-element.183, bf16[27,220,660]{1,2,0:T(8,128)(2,1)} %get-tuple-element.202, s32[]{:T(128)S(6)} %copy.93), kind=kOutput, calls=%fused_computation.2.clone.1 | convolution fusion | flops 298946560 | bytes 6214661 | tf_op jit(solution)/shard_map/while/body/eval_jaxpr/dot_general | solution.py:78
  131.6 3.9 gather_fusion
  135.5 4.1 %select_add_fusion.2 = f32[1024,660]{0,1:T(8,128)} fusion(f32[1024,660]{0,1:T(8,128)} %get-tuple-element.192, pred[]{:T(512)S(6)} %compare.5, bf16[1024,220]{1,0:T(8,128)(2,1)S(1)} %gather_fusion, pred[1024]{0:T(1024)(128)(4,1)S(1)} %get-tuple-element.183, bf16[27,220,660]{1,2,0:T(8,128)(2,1)} %get-tuple-element.202, s32[]{:T(128)S(6)} %copy.93), kind=kOutput, calls=%fused_computation.2.clone.1 | convolution fusion | flops 298946560 | bytes 6214661 | tf_op jit(solution)/shard_map/while/body/eval_jaxpr/dot_general | solution.py:78
  140.4 3.9 gather_fusion
  144.3 4.1 %select_add_fusion.2 = f32[1024,660]{0,1:T(8,128)} fusion(f32[1024,660]{0,1:T(8,128)} %get-tuple-element.192, pred[]{:T(512)S(6)} %compare.5, bf16[1024,220]{1,0:T(8,128)(2,1)S(1)} %gather_fusion, pred[1024]{0:T(1024)(128)(4,1)S(1)} %get-tuple-element.183, bf16[27,220,660]{1,2,0:T(8,128)(2,1)} %get-tuple-element.202, s32[]{:T(128)S(6)} %copy.93), kind=kOutput, calls=%fused_computation.2.clone.1 | convolution fusion | flops 298946560 | bytes 6214661 | tf_op jit(solution)/shard_map/while/body/eval_jaxpr/dot_general | solution.py:78
  149.2 3.9 gather_fusion
  153.2 4.1 %select_add_fusion.2 = f32[1024,660]{0,1:T(8,128)} fusion(f32[1024,660]{0,1:T(8,128)} %get-tuple-element.192, pred[]{:T(512)S(6)} %compare.5, bf16[1024,220]{1,0:T(8,128)(2,1)S(1)} %gather_fusion, pred[1024]{0:T(1024)(128)(4,1)S(1)} %get-tuple-element.183, bf16[27,220,660]{1,2,0:T(8,128)(2,1)} %get-tuple-element.202, s32[]{:T(128)S(6)} %copy.93), kind=kOutput, calls=%fused_computation.2.clone.1 | convolution fusion | flops 298946560 | bytes 6214661 | tf_op jit(solution)/shard_map/while/body/eval_jaxpr/dot_general | solution.py:78
  158.0 3.9 gather_fusion
  162.0 4.1 %select_add_fusion.2 = f32[1024,660]{0,1:T(8,128)} fusion(f32[1024,660]{0,1:T(8,128)} %get-tuple-element.192, pred[]{:T(512)S(6)} %compare.5, bf16[1024,220]{1,0:T(8,128)(2,1)S(1)} %gather_fusion, pred[1024]{0:T(1024)(128)(4,1)S(1)} %get-tuple-element.183, bf16[27,220,660]{1,2,0:T(8,128)(2,1)} %get-tuple-element.202, s32[]{:T(128)S(6)} %copy.93), kind=kOutput, calls=%fused_computation.2.clone.1 | convolution fusion | flops 298946560 | bytes 6214661 | tf_op jit(solution)/shard_map/while/body/eval_jaxpr/dot_general | solution.py:78
  166.8 3.9 gather_fusion
  170.8 4.1 %select_add_fusion.2 = f32[1024,660]{0,1:T(8,128)} fusion(f32[1024,660]{0,1:T(8,128)} %get-tuple-element.192, pred[]{:T(512)S(6)} %compare.5, bf16[1024,220]{1,0:T(8,128)(2,1)S(1)} %gather_fusion, pred[1024]{0:T(1024)(128)(4,1)S(1)} %get-tuple-element.183, bf16[27,220,660]{1,2,0:T(8,128)(2,1)} %get-tuple-element.202, s32[]{:T(128)S(6)} %copy.93), kind=kOutput, calls=%fused_computation.2.clone.1 | convolution fusion | flops 298946560 | bytes 6214661 | tf_op jit(solution)/shard_map/while/body/eval_jaxpr/dot_general | solution.py:78
  175.7 3.9 gather_fusion
  179.6 4.1 %select_add_fusion.2 = f32[1024,660]{0,1:T(8,128)} fusion(f32[1024,660]{0,1:T(8,128)} %get-tuple-element.192, pred[]{:T(512)S(6)} %compare.5, bf16[1024,220]{1,0:T(8,128)(2,1)S(1)} %gather_fusion, pred[1024]{0:T(1024)(128)(4,1)S(1)} %get-tuple-element.183, bf16[27,220,660]{1,2,0:T(8,128)(2,1)} %get-tuple-element.202, s32[]{:T(128)S(6)} %copy.93), kind=kOutput, calls=%fused_computation.2.clone.1 | convolution fusion | flops 298946560 | bytes 6214661 | tf_op jit(solution)/shard_map/while/body/eval_jaxpr/dot_general | solution.py:78
  188.4 4.1 %select_add_fusion.2 = f32[1024,660]{0,1:T(8,128)} fusion(f32[1024,660]{0,1:T(8,128)} %get-tuple-element.192, pred[]{:T(512)S(6)} %compare.5, bf16[1024,220]{1,0:T(8,128)(2,1)S(1)} %gather_fusion, pred[1024]{0:T(1024)(128)(4,1)S(1)} %get-tuple-element.183, bf16[27,220,660]{1,2,0:T(8,128)(2,1)} %get-tuple-element.202, s32[]{:T(128)S(6)} %copy.93), kind=kOutput, calls=%fused_computation.2.clone.1 | convolution fusion | flops 298946560 | bytes 6214661 | tf_op jit(solution)/shard_map/while/body/eval_jaxpr/dot_general | solution.py:78
  197.2 4.1 %select_add_fusion.2 = f32[1024,660]{0,1:T(8,128)} fusion(f32[1024,660]{0,1:T(8,128)} %get-tuple-element.192, pred[]{:T(512)S(6)} %compare.5, bf16[1024,220]{1,0:T(8,128)(2,1)S(1)} %gather_fusion, pred[1024]{0:T(1024)(128)(4,1)S(1)} %get-tuple-element.183, bf16[27,220,660]{1,2,0:T(8,128)(2,1)} %get-tuple-element.202, s32[]{:T(128)S(6)} %copy.93), kind=kOutput, calls=%fused_computation.2.clone.1 | convolution fusion | flops 298946560 | bytes 6214661 | tf_op jit(solution)/shard_map/while/body/eval_jaxpr/dot_general | solution.py:78
  206.1 4.1 %select_add_fusion.2 = f32[1024,660]{0,1:T(8,128)} fusion(f32[1024,660]{0,1:T(8,128)} %get-tuple-element.192, pred[]{:T(512)S(6)} %compare.5, bf16[1024,220]{1,0:T(8,128)(2,1)S(1)} %gather_fusion, pred[1024]{0:T(1024)(128)(4,1)S(1)} %get-tuple-element.183, bf16[27,220,660]{1,2,0:T(8,128)(2,1)} %get-tuple-element.202, s32[]{:T(128)S(6)} %copy.93), kind=kOutput, calls=%fused_computation.2.clone.1 | convolution fusion | flops 298946560 | bytes 6214661 | tf_op jit(solution)/shard_map/while/body/eval_jaxpr/dot_general | solution.py:78
  214.9 4.1 %select_add_fusion.2 = f32[1024,660]{0,1:T(8,128)} fusion(f32[1024,660]{0,1:T(8,128)} %get-tuple-element.192, pred[]{:T(512)S(6)} %compare.5, bf16[1024,220]{1,0:T(8,128)(2,1)S(1)} %gather_fusion, pred[1024]{0:T(1024)(128)(4,1)S(1)} %get-tuple-element.183, bf16[27,220,660]{1,2,0:T(8,128)(2,1)} %get-tuple-element.202, s32[]{:T(128)S(6)} %copy.93), kind=kOutput, calls=%fused_computation.2.clone.1 | convolution fusion | flops 298946560 | bytes 6214661 | tf_op jit(solution)/shard_map/while/body/eval_jaxpr/dot_general | solution.py:78
  223.7 4.1 %select_add_fusion.2 = f32[1024,660]{0,1:T(8,128)} fusion(f32[1024,660]{0,1:T(8,128)} %get-tuple-element.192, pred[]{:T(512)S(6)} %compare.5, bf16[1024,220]{1,0:T(8,128)(2,1)S(1)} %gather_fusion, pred[1024]{0:T(1024)(128)(4,1)S(1)} %get-tuple-element.183, bf16[27,220,660]{1,2,0:T(8,128)(2,1)} %get-tuple-element.202, s32[]{:T(128)S(6)} %copy.93), kind=kOutput, calls=%fused_computation.2.clone.1 | convolution fusion | flops 298946560 | bytes 6214661 | tf_op jit(solution)/shard_map/while/body/eval_jaxpr/dot_general | solution.py:78
  232.5 4.1 %select_add_fusion.2 = f32[1024,660]{0,1:T(8,128)} fusion(f32[1024,660]{0,1:T(8,128)} %get-tuple-element.192, pred[]{:T(512)S(6)} %compare.5, bf16[1024,220]{1,0:T(8,128)(2,1)S(1)} %gather_fusion, pred[1024]{0:T(1024)(128)(4,1)S(1)} %get-tuple-element.183, bf16[27,220,660]{1,2,0:T(8,128)(2,1)} %get-tuple-element.202, s32[]{:T(128)S(6)} %copy.93), kind=kOutput, calls=%fused_computation.2.clone.1 | convolution fusion | flops 298946560 | bytes 6214661 | tf_op jit(solution)/shard_map/while/body/eval_jaxpr/dot_general | solution.py:78
  241.3 4.1 %select_add_fusion.2 = f32[1024,660]{0,1:T(8,128)} fusion(f32[1024,660]{0,1:T(8,128)} %get-tuple-element.192, pred[]{:T(512)S(6)} %compare.5, bf16[1024,220]{1,0:T(8,128)(2,1)S(1)} %gather_fusion, pred[1024]{0:T(1024)(128)(4,1)S(1)} %get-tuple-element.183, bf16[27,220,660]{1,2,0:T(8,128)(2,1)} %get-tuple-element.202, s32[]{:T(128)S(6)} %copy.93), kind=kOutput, calls=%fused_computation.2.clone.1 | convolution fusion | flops 298946560 | bytes 6214661 | tf_op jit(solution)/shard_map/while/body/eval_jaxpr/dot_general | solution.py:78
  250.1 4.1 %select_add_fusion.2 = f32[1024,660]{0,1:T(8,128)} fusion(f32[1024,660]{0,1:T(8,128)} %get-tuple-element.192, pred[]{:T(512)S(6)} %compare.5, bf16[1024,220]{1,0:T(8,128)(2,1)S(1)} %gather_fusion, pred[1024]{0:T(1024)(128)(4,1)S(1)} %get-tuple-element.183, bf16[27,220,660]{1,2,0:T(8,128)(2,1)} %get-tuple-element.202, s32[]{:T(128)S(6)} %copy.93), kind=kOutput, calls=%fused_computation.2.clone.1 | convolution fusion | flops 298946560 | bytes 6214661 | tf_op jit(solution)/shard_map/while/body/eval_jaxpr/dot_general | solution.py:78
  259.0 4.1 %select_add_fusion.2 = f32[1024,660]{0,1:T(8,128)} fusion(f32[1024,660]{0,1:T(8,128)} %get-tuple-element.192, pred[]{:T(512)S(6)} %compare.5, bf16[1024,220]{1,0:T(8,128)(2,1)S(1)} %gather_fusion, pred[1024]{0:T(1024)(128)(4,1)S(1)} %get-tuple-element.183, bf16[27,220,660]{1,2,0:T(8,128)(2,1)} %get-tuple-element.202, s32[]{:T(128)S(6)} %copy.93), kind=kOutput, calls=%fused_computation.2.clone.1 | convolution fusion | flops 298946560 | bytes 6214661 | tf_op jit(solution)/shard_map/while/body/eval_jaxpr/dot_general | solution.py:78
  267.8 4.1 %select_add_fusion.2 = f32[1024,660]{0,1:T(8,128)} fusion(f32[1024,660]{0,1:T(8,128)} %get-tuple-element.192, pred[]{:T(512)S(6)} %compare.5, bf16[1024,220]{1,0:T(8,128)(2,1)S(1)} %gather_fusion, pred[1024]{0:T(1024)(128)(4,1)S(1)} %get-tuple-element.183, bf16[27,220,660]{1,2,0:T(8,128)(2,1)} %get-tuple-element.202, s32[]{:T(128)S(6)} %copy.93), kind=kOutput, calls=%fused_computation.2.clone.1 | convolution fusion | flops 298946560 | bytes 6214661 | tf_op jit(solution)/shard_map/while/body/eval_jaxpr/dot_general | solution.py:78
  276.6 4.1 %select_add_fusion.2 = f32[1024,660]{0,1:T(8,128)} fusion(f32[1024,660]{0,1:T(8,128)} %get-tuple-element.192, pred[]{:T(512)S(6)} %compare.5, bf16[1024,220]{1,0:T(8,128)(2,1)S(1)} %gather_fusion, pred[1024]{0:T(1024)(128)(4,1)S(1)} %get-tuple-element.183, bf16[27,220,660]{1,2,0:T(8,128)(2,1)} %get-tuple-element.202, s32[]{:T(128)S(6)} %copy.93), kind=kOutput, calls=%fused_computation.2.clone.1 | convolution fusion | flops 298946560 | bytes 6214661 | tf_op jit(solution)/shard_map/while/body/eval_jaxpr/dot_general | solution.py:78
  285.4 4.1 %select_add_fusion.2 = f32[1024,660]{0,1:T(8,128)} fusion(f32[1024,660]{0,1:T(8,128)} %get-tuple-element.192, pred[]{:T(512)S(6)} %compare.5, bf16[1024,220]{1,0:T(8,128)(2,1)S(1)} %gather_fusion, pred[1024]{0:T(1024)(128)(4,1)S(1)} %get-tuple-element.183, bf16[27,220,660]{1,2,0:T(8,128)(2,1)} %get-tuple-element.202, s32[]{:T(128)S(6)} %copy.93), kind=kOutput, calls=%fused_computation.2.clone.1 | convolution fusion | flops 298946560 | bytes 6214661 | tf_op jit(solution)/shard_map/while/body/eval_jaxpr/dot_general | solution.py:78
  294.2 4.1 %select_add_fusion.2 = f32[1024,660]{0,1:T(8,128)} fusion(f32[1024,660]{0,1:T(8,128)} %get-tuple-element.192, pred[]{:T(512)S(6)} %compare.5, bf16[1024,220]{1,0:T(8,128)(2,1)S(1)} %gather_fusion, pred[1024]{0:T(1024)(128)(4,1)S(1)} %get-tuple-element.183, bf16[27,220,660]{1,2,0:T(8,128)(2,1)} %get-tuple-element.202, s32[]{:T(128)S(6)} %copy.93), kind=kOutput, calls=%fused_computation.2.clone.1 | convolution fusion | flops 298946560 | bytes 6214661 | tf_op jit(solution)/shard_map/while/body/eval_jaxpr/dot_general | solution.py:78
  303.0 4.1 %select_add_fusion.2 = f32[1024,660]{0,1:T(8,128)} fusion(f32[1024,660]{0,1:T(8,128)} %get-tuple-element.192, pred[]{:T(512)S(6)} %compare.5, bf16[1024,220]{1,0:T(8,128)(2,1)S(1)} %gather_fusion, pred[1024]{0:T(1024)(128)(4,1)S(1)} %get-tuple-element.183, bf16[27,220,660]{1,2,0:T(8,128)(2,1)} %get-tuple-element.202, s32[]{:T(128)S(6)} %copy.93), kind=kOutput, calls=%fused_computation.2.clone.1 | convolution fusion | flops 298946560 | bytes 6214661 | tf_op jit(solution)/shard_map/while/body/eval_jaxpr/dot_general | solution.py:78
  311.9 4.1 %select_add_fusion.2 = f32[1024,660]{0,1:T(8,128)} fusion(f32[1024,660]{0,1:T(8,128)} %get-tuple-element.192, pred[]{:T(512)S(6)} %compare.5, bf16[1024,220]{1,0:T(8,128)(2,1)S(1)} %gather_fusion, pred[1024]{0:T(1024)(128)(4,1)S(1)} %get-tuple-element.183, bf16[27,220,660]{1,2,0:T(8,128)(2,1)} %get-tuple-element.202, s32[]{:T(128)S(6)} %copy.93), kind=kOutput, calls=%fused_computation.2.clone.1 | convolution fusion | flops 298946560 | bytes 6214661 | tf_op jit(solution)/shard_map/while/body/eval_jaxpr/dot_general | solution.py:78
  320.7 4.1 %select_add_fusion.2 = f32[1024,660]{0,1:T(8,128)} fusion(f32[1024,660]{0,1:T(8,128)} %get-tuple-element.192, pred[]{:T(512)S(6)} %compare.5, bf16[1024,220]{1,0:T(8,128)(2,1)S(1)} %gather_fusion, pred[1024]{0:T(1024)(128)(4,1)S(1)} %get-tuple-element.183, bf16[27,220,660]{1,2,0:T(8,128)(2,1)} %get-tuple-element.202, s32[]{:T(128)S(6)} %copy.93), kind=kOutput, calls=%fused_computation.2.clone.1 | convolution fusion | flops 298946560 | bytes 6214661 | tf_op jit(solution)/shard_map/while/body/eval_jaxpr/dot_general | solution.py:78
  330.4 4.5 %fusion.11 = bf16[2048,660]{0,1:T(8,128)(2,1)} fusion(bf16[1024,660]{1,0:T(8,128)(2,1)S(1)} %fusion.13, s32[1024]{0:T(1024)S(1)} %add_add_fusion), kind=kOutput, calls=%fused_computation.18 | convolution fusion | flops 2771689472 | bytes 4059136 | tf_op jit(solution)/shard_map/dot_general | solution.py:116
  334.9 4.6 %copy.51 = bf16[2048,660]{1,0:T(8,128)(2,1)} copy(bf16[2048,660]{0,1:T(8,128)(2,1)} %fusion.11) | data formatting | bytes 5406720 | tf_op jit(solution)/shard_map/convert_element_type | solution.py:116
  339.5 6.1 %all-to-all-start.1 = ((bf16[128,16,660]{2,1,0:T(8,128)(2,1)}), bf16[128,16,660]{2,1,0:T(8,128)(2,1)}, u32[]{:S(2)}, u32[]{:S(2)}) async-start(bf16[128,16,660]{2,1,0:T(8,128)(2,1)} %bitcast.102), calls=%async_computation.1 | async-start | bytes 6291456 | tf_op jit(solution)/shard_map/all_to_all | solution.py:123
  351.8 6.4 %fusion.28 = f32[2048,1024]{1,0:T(8,128)} fusion(bf16[220,1024]{1,0:T(8,128)(2,1)S(1)} %copy-done.4, bf16[2048,220]{0,1:T(8,128)(2,1)} %fusion.41, bf16[2048,220]{0,1:T(8,128)(2,1)} %fusion.19, bf16[2048,220]{1,0:T(8,128)(2,1)S(1)} %gather_fusion.1, pred[2048]{0:T(1024)(128)(4,1)S(1)} %get-tuple-element.144, pred[2048]{0:T(1024)(128)(4,1)S(1)} %get-tuple-element.139, ...), kind=kOutput, calls=%fused_computation.46 | convolution fusion | flops 1121894400 | bytes 11643424 | tf_op jit(solution)/shard_map/dot_general | solution.py:33
  360.0 26.9 %all-to-all-done.1 = bf16[128,16,660]{2,1,0:T(8,128)(2,1)} async-done(((bf16[128,16,660]{2,1,0:T(8,128)(2,1)}), bf16[128,16,660]{2,1,0:T(8,128)(2,1)}, u32[]{:S(2)}, u32[]{:S(2)}) %all-to-all-start.1) | async-done | bytes 2703392 | tf_op jit(solution)/shard_map/all_to_all | solution.py:123
  386.9 10.8 %dot_general.78 = bf16[2048,3,220]{2,1,0:T(4,128)(2,1)} reshape(bf16[128,16,660]{2,1,0:T(8,128)(2,1)} %all-to-all-done.1) | data formatting | bytes 5406720 | tf_op jit(solution)/shard_map/dot_general | solution.py:35
  400.9 4.6 %fusion.26 = bf16[2048,256]{1,0:T(8,128)(2,1)} fusion(f32[2048,1024]{1,0:T(8,128)} %fusion.28, f32[2048,3,256]{2,0,1:T(8,128)S(1)} %fusion.14, f32[2048]{0:T(1024)S(1)} %reshape.132), kind=kLoop, calls=%fused_computation.38 | loop fusion | flops 4718592 | bytes 15736832 | tf_op jit(solution)/shard_map/convert_element_type | solution.py:44
  (156 shorter events, 127.7 us)
Async XLA Ops:
  0.6 74.4 %copy-start = (bf16[8,56,220]{2,1,0:T(8,128)(2,1)S(1)}, bf16[8,56,220]{2,1,0:T(8,128)(2,1)}, u32[]{:S(2)}) copy-start(bf16[8,56,220]{2,1,0:T(8,128)(2,1)} %param.23) | copy-start | bytes 591364
  0.6 10.6 %copy-start.14 = (s32[1024,1]{0,1:T(1,128)S(1)}, s32[1024,1]{0,1:T(1,128)}, u32[]{:S(2)}) copy-start(s32[1024,1]{0,1:T(1,128)} %param.24) | copy-start | bytes 12292
  3.6 82.3 %collective-permute-start.1 = (bf16[1024,220]{1,0:T(8,128)(2,1)}, bf16[1024,220]{1,0:T(8,128)(2,1)}, u32[]{:S(2)}, u32[]{:S(2)}) collective-permute-start(bf16[1024,220]{1,0:T(8,128)(2,1)} %multiply_convert_fusion), channel_id=1, source_target_pairs={{1,0},{2,1},{3,2},{4,3},{5,4},{6,5},{7,6},{8,7},{9,8},{10,9},{11,1... | collective-permute-start | bytes 1351688 | tf_op jit(solution)/shard_map/ppermute | solution.py:18
  6.9 79.0 %collective-permute-start = (bf16[1024,220]{1,0:T(8,128)(2,1)}, bf16[1024,220]{1,0:T(8,128)(2,1)}, u32[]{:S(2)}, u32[]{:S(2)}) collective-permute-start(bf16[1024,220]{1,0:T(8,128)(2,1)} %multiply_convert_fusion), channel_id=1, source_target_pairs={{0,1},{1,2},{2,3},{3,4},{4,5},{5,6},{6,7},{7,8},{8,9},{9,10},{10,1... | collective-permute-start | bytes 1351688 | tf_op jit(solution)/shard_map/ppermute | solution.py:15
  11.3 16.9 %copy-start.16 = (s32[2048]{0:T(1024)S(1)}, s32[2048]{0:T(1024)}, u32[]{:S(2)}) copy-start(s32[2048]{0:T(1024)} %param.26) | copy-start | bytes 24580
  11.3 16.9 %copy-start.15 = (s32[2048]{0:T(1024)S(1)}, s32[2048]{0:T(1024)}, u32[]{:S(2)}) copy-start(s32[2048]{0:T(1024)} %param.27) | copy-start | bytes 24580
  11.3 16.9 %copy-start.3 = (bf16[2048,220]{0,1:T(8,128)(2,1)S(1)}, bf16[2048,220]{0,1:T(8,128)(2,1)}, u32[]{:S(2)}) copy-start(bf16[2048,220]{0,1:T(8,128)(2,1)} %param.25) | copy-start | bytes 2703364
  13.9 325.6 %all-to-all-start = ((bf16[128,1,16]{2,1,0:T(2,128)(2,1)}), bf16[128,1,16]{2,1,0:T(2,128)(2,1)S(1)}, u32[]{:S(2)}, u32[]{:S(2)}) async-start(bf16[128,1,16]{2,1,0:T(2,128)(2,1)} %all_to_all.12), calls=%async_computation | async-start | bytes 131072 | tf_op jit(solution)/shard_map/all_to_all | solution.py:130
  28.8 45.1 %copy-start.13 = (f32[56,168]{1,0:T(8,128)S(1)}, f32[56,168]{1,0:T(8,128)}, u32[]{:S(2)}) copy-start(f32[56,168]{1,0:T(8,128)} %param.21) | copy-start | bytes 112900
  28.8 46.5 %copy-start.12 = (s32[1024,27]{0,1:T(8,128)S(1)}, s32[1024,27]{0,1:T(8,128)}, u32[]{:S(2)}) copy-start(s32[1024,27]{0,1:T(8,128)} %param.18) | copy-start | bytes 331780
  76.0 7.5 %copy-start.2 = (bf16[8,220,220]{2,0,1:T(8,128)(2,1)S(1)}, bf16[8,220,220]{2,0,1:T(8,128)(2,1)}, u32[]{:S(2)}) copy-start(bf16[8,220,220]{2,0,1:T(8,128)(2,1)} %param.28) | copy-start | bytes 2323204
  339.5 6.1 %copy-start.9 = (bf16[1,220,220]{2,0,1:T(2,128)(2,1)S(1)}, bf16[1,220,220]{2,0,1:T(2,128)(2,1)}, u32[]{:S(2)}) copy-start(bf16[1,220,220]{2,0,1:T(2,128)(2,1)} %get-tuple-element.132) | copy-start | bytes 290404
  339.5 6.6 %copy-start.8 = (bf16[1,220,220]{2,0,1:T(2,128)(2,1)S(1)}, bf16[1,220,220]{2,0,1:T(2,128)(2,1)}, u32[]{:S(2)}) copy-start(bf16[1,220,220]{2,0,1:T(2,128)(2,1)} %get-tuple-element.133) | copy-start | bytes 290404
  339.5 47.4 %all-to-all-start.1 = ((bf16[128,16,660]{2,1,0:T(8,128)(2,1)}), bf16[128,16,660]{2,1,0:T(8,128)(2,1)}, u32[]{:S(2)}, u32[]{:S(2)}) async-start(bf16[128,16,660]{2,1,0:T(8,128)(2,1)} %bitcast.102), calls=%async_computation.1 | async-start | bytes 6291456 | tf_op jit(solution)/shard_map/all_to_all | solution.py:123
  345.6 1.1 copy-start.7
  345.6 1.6 copy-start.6
  346.1 1.6 copy-start.5
  346.7 2.5 copy-start.11
  349.2 0.9 copy-start.10
  349.9 2.0 copy-start.4
  400.9 4.6 %copy-start.1 = (bf16[8,56,220]{2,1,0:T(8,128)(2,1)S(1)}, bf16[8,56,220]{2,1,0:T(8,128)(2,1)}, u32[]{:S(2)}) copy-start(bf16[8,56,220]{2,1,0:T(8,128)(2,1)} %param.23) | copy-start | bytes 591364
